TPU v7x, 256 devices: a whole 4x4x8 slice. The times are simulated.
256 devices in a mesh: replica: 16 (over z_lo, x), fsdp: 16 (over y, z_hi, core).
Axes of the slice: x: 4, y: 4, z: 8 (z_hi: 2, z_lo: 4; z = z_hi * 4 + z_lo), core: 2. Of those that a mesh axis runs over, the one named last changes fastest.
Arguments:
- base: float32 [8192, 1024], P('fsdp'), may hold values from -6 to 6
- local: bfloat16 [16, 8192, 1024], P('replica', 'fsdp'), may hold values from -6 to 6
- momentum: float32 [8192, 1024], P('fsdp'), may hold values from -6 to 6
- tokens: bfloat16 [16, 2048, 8192], P('replica', 'fsdp'), may hold values from -6 to 6
- mask_embed: bfloat16 [8192], replicated, may hold values from -6 to 6
- mask_pos: int32 [16, 1, 768], P('replica'), may hold values from 0 to 2047, as said below
- cotangent: bfloat16 [16, 2048, 1024], P('replica', 'fsdp'), may hold values from -6 to 6
Outputs:
- new_momentum: bfloat16 [8192, 1024], P('fsdp')
- stepped: bfloat16 [16, 8192, 1024], P('replica', 'fsdp')
Inputs may be any that keep to these rules, and one draw needn't show every extreme that they name: `mask_pos`: each row holds 768 different positions of its sequence.
All inputs are finite; a program needn't handle non-finite values. Where the computation divides by a largest or mean magnitude, that divisor is 1e-20 or more.
Results may differ from a plain program's by a relative error of at most 0.008.
Values may be sent and summed in bfloat16 or wider, within the bound.
A program may use at most 128 MiB of HBM per device.

v0:
```python
import jax
import jax.numpy as jnp
from jax import lax
from jax.sharding import PartitionSpec as P

D = 8192
QBLOCK = 128
LENGTH = 2048
momentum_decay = 0.9
outer_rate = 0.7
inner_rate = 0.5


def body(base, local, momentum, tokens, mask_embed, mask_pos, cotangent):
    row_count, col_count = base.shape
    drift = base - local[0].astype(jnp.float32)
    blocks = drift.reshape(row_count, col_count // QBLOCK, QBLOCK)
    scales = (jnp.max(jnp.abs(blocks), axis=2, keepdims=True) + 1e-06).astype(jnp.bfloat16)
    code_vals = (blocks / scales.astype(jnp.float32)).astype(jnp.bfloat16)
    replicas = lax.axis_size("replica")
    dequant = (code_vals.astype(jnp.float32) * scales.astype(jnp.float32)).reshape(
        row_count, col_count
    )
    outer_grad = lax.psum(dequant, "replica") / replicas
    momentum_next = momentum_decay * momentum + outer_grad
    renewed = base - outer_rate * (outer_grad + momentum_decay * momentum_next)
    tok_rows = tokens.shape[1]
    offset = lax.axis_index("fsdp") * tok_rows
    places = offset + jnp.arange(tok_rows, dtype=jnp.int32)
    sequence = places // LENGTH
    position = places % LENGTH
    seq_ids = jnp.arange(mask_pos.shape[1], dtype=jnp.int32)
    matches = (mask_pos[0][None, :, :] == position[:, None, None]) & (
        sequence[:, None, None] == seq_ids[None, :, None]
    )
    masked = jnp.any(matches, axis=(1, 2))
    inputs = jnp.where(masked[:, None], mask_embed[None, :], tokens[0])
    upstream = cotangent[0]
    own_columns = lax.all_to_all(inputs, "fsdp", split_axis=1, concat_axis=0, tiled=True)
    all_upstream = lax.all_gather(upstream, "fsdp", axis=0, tiled=True)
    groups = lax.axis_size("fsdp")
    group_in = own_columns.reshape(groups, tok_rows, row_count)
    group_up = all_upstream.reshape(groups, tok_rows, col_count)

    def add_group(total, pair):
        term = lax.dot_general(
            pair[0], pair[1], (((0,), (0,)), ((), ())), preferred_element_type=jnp.float32
        )
        return (total + term.astype(jnp.bfloat16).astype(jnp.float32), None)

    grad_sum, _ = lax.scan(
        add_group, jnp.zeros((row_count, col_count), jnp.float32), (group_in, group_up)
    )
    gradient = grad_sum * D ** (-0.5)
    stepped = (renewed - inner_rate * gradient).astype(jnp.bfloat16)
    return (momentum_next.astype(jnp.bfloat16), stepped[None])


def solution(mesh):
    in_specs = (
        P("fsdp", None),
        P("replica", "fsdp", None),
        P("fsdp", None),
        P("replica", "fsdp", None),
        P(),
        P("replica", None, None),
        P("replica", "fsdp", None),
    )
    out_specs = (P("fsdp", None), P("replica", "fsdp", None))
    return jax.shard_map(body, mesh=mesh, in_specs=in_specs, out_specs=out_specs, check_vma=False)
```

profile of v0, /device:TPU:8, one launch (start us, length us, event | category | flops | bytes accessed | tf_op | source)
XLA Modules:
  0.0 255.8 jit_solution(18432817212518945594)
XLA Ops:
  8.8 3.2 %copy.18 = bf16[1,128,8192]{1,2,0:T(8,128)(2,1)S(1)} copy(bf16[1,128,8192]{2,1,0:T(8,128)(2,1)} %param.12) | data formatting | bytes 4194304 | tf_op args[3]
  12.3 2.2 broadcast_select_fusion
  14.5 11.8 %all-to-all-start = ((bf16[128,16,512]{0,2,1:T(8,128)(2,1)}), bf16[128,16,512]{0,2,1:T(8,128)(2,1)}, u32[]{:S(2)}, u32[]{:S(2)}) async-start(bf16[128,16,512]{0,2,1:T(8,128)(2,1)} %broadcast_select_fusion), calls=%async_computation | async-start | bytes 4194304 | tf_op jit(solution)/shard_map/all_to_all | solution.py:39
  26.8 1.8 copy.21
  28.6 2.2 reduce_max.9
  31.7 2.1 bitcast_multiply_fusion
  33.9 46.6 %all-to-all-done = bf16[128,16,512]{0,2,1:T(8,128)(2,1)} async-done(((bf16[128,16,512]{0,2,1:T(8,128)(2,1)}), bf16[128,16,512]{0,2,1:T(8,128)(2,1)}, u32[]{:S(2)}, u32[]{:S(2)}) %all-to-all-start) | async-done | bytes 2097184 | tf_op jit(solution)/shard_map/all_to_all | solution.py:39
  80.4 41.1 %all-gather.3.cloned.1.call-done = bf16[1,2048,1024]{2,1,0:T(8,128)(2,1)} async-done(((bf16[1,128,1024]{2,1,0:T(8,128)(2,1)}), bf16[1,2048,1024]{2,1,0:T(8,128)(2,1)}) %all-gather.3.cloned.1.call-update) | async-done | bytes 4194320 | tf_op jit(solution)/shard_map/all_gather | solution.py:40
  121.5 27.8 %while.11 = (s32[]{:T(128)}, f32[512,1024]{1,0:T(8,128)S(1)}, bf16[16,128,512]{1,2,0:T(8,128)(2,1)}, bf16[16,128,1024]{2,1,0:T(8,128)(2,1)}, s32[]{:T(128)}, /*index=5*/s32[]{:T(128)}) while((s32[]{:T(128)}, f32[512,1024]{1,0:T(8,128)S(1)}, bf16[16,128,512]{1,2,0:T(8,128)(2,1)}, bf16[16,128,1024]{2,1,0:T(8,128)(2,1)}, s32[]{:T(128)}, ...), condition=%wide.region_4.5_spmd.clone, body=%wide.region_3.4_spmd.clone.sunk | while | flops 136314880 | bytes 4588623 | solution.py:51
  123.3 1.7 select_add_fusion.2
  125.0 1.7 select_add_fusion.2
  126.7 1.7 select_add_fusion.2
  128.5 1.7 select_add_fusion.2
  130.2 1.7 select_add_fusion.2
  132.0 1.7 select_add_fusion.2
  133.7 1.7 select_add_fusion.2
  135.4 1.7 select_add_fusion.2
  137.2 1.7 select_add_fusion.2
  138.9 1.7 select_add_fusion.2
  142.4 1.7 select_add_fusion.2
  144.1 1.7 select_add_fusion.2
  147.6 1.7 select_add_fusion.2
  149.4 93.7 %all-reduce.2.cloned.1.call-done = f32[512,1024]{1,0:T(8,128)} async-done(((f32[512,1024]{1,0:T(8,128)}), f32[512,1024]{1,0:T(8,128)}) %all-reduce.2.cloned.1.call-update) | async-done | bytes 2097168 | tf_op jit(solution)/shard_map/psum | solution.py:24
  243.1 5.3 %fusion.7 = (bf16[1,512,1024]{2,1,0:T(8,128)(2,1)}, bf16[512,1024]{1,0:T(8,128)(2,1)}) fusion(f32[512,1024]{1,0:T(8,128)S(1)} %get-tuple-element.24, f32[512,1024]{1,0:T(8,128)} %param.9, f32[512,1024]{1,0:T(8,128)} %param.11, f32[512,1024]{1,0:T(8,128)} %all-reduce.2.cloned.1.call-done), kind=kLoop, calls=%fused_computation.16 | loop fusion | flops 5767168 | bytes 10485760 | tf_op jit(solution)/shard_map/broadcast_in_dim | solution.py:56
  (26 shorter events, 7.4 us)
Async XLA Ops:
  8.0 113.5 %all-gather.3.cloned.1.call-start = ((), (), s32[]{:S(2)}) async-start(), calls=%async_computation.2 | async-start | bytes 4456448 | tf_op jit(solution)/shard_map/all_gather | solution.py:40
  8.7 3.3 %copy-start.2 = (bf16[8192]{0:T(1024)(128)(2,1)S(1)}, bf16[8192]{0:T(1024)(128)(2,1)}, u32[]{:S(2)}) copy-start(bf16[8192]{0:T(1024)(128)(2,1)} %param.13) | copy-start | bytes 49156
  8.7 3.3 %copy-start.3 = (s32[1,1,768]{2,1,0:T(1,128)S(1)}, s32[1,1,768]{2,1,0:T(1,128)}, u32[]{:S(2)}) copy-start(s32[1,1,768]{2,1,0:T(1,128)} %param.14) | copy-start | bytes 9220
  14.5 11.9 %copy-start = (f32[512,1024]{1,0:T(8,128)S(1)}, f32[512,1024]{1,0:T(8,128)}, u32[]{:S(2)}) copy-start(f32[512,1024]{1,0:T(8,128)} %param.9) | copy-start | bytes 6291460
  14.5 11.9 %copy-start.1 = (bf16[1,512,1024]{2,1,0:T(8,128)(2,1)S(1)}, bf16[1,512,1024]{2,1,0:T(8,128)(2,1)}, u32[]{:S(2)}) copy-start(bf16[1,512,1024]{2,1,0:T(8,128)(2,1)} %param.10) | copy-start | bytes 3145732
  14.5 65.9 %all-to-all-start = ((bf16[128,16,512]{0,2,1:T(8,128)(2,1)}), bf16[128,16,512]{0,2,1:T(8,128)(2,1)}, u32[]{:S(2)}, u32[]{:S(2)}) async-start(bf16[128,16,512]{0,2,1:T(8,128)(2,1)} %broadcast_select_fusion), calls=%async_computation | async-start | bytes 4194304 | tf_op jit(solution)/shard_map/all_to_all | solution.py:39
  26.4 216.7 %all-reduce.2.cloned.1.call-start = ((), (), s32[]{:S(2)}) async-start(), calls=%async_computation.1 | async-start | bytes 4194304 | tf_op jit(solution)/shard_map/psum | solution.py:24
Sparse Core Ops, SparseCore 0:
  11.5 109.9 all-gather.2
Sparse Core Ops, SparseCore 1:
  33.9 209.1 all-reduce.1
where the time goes:
time: 256 us
  waiting for transfers between devices  182 us (71%)
  matrix products  27.5 us (11%)
  between operations  15.6 us (6%)
  other arithmetic  12.4 us (5%)
  starting transfers between devices  11.9 us (5%)
  local copies, waits for them, and re-layouts  5.93 us (2%)
    psum x1, waiting for transfers between devices, body(): outer_grad = lax.psum(dequant, 'replica') / replicas  93.7 us
    all_to_all x1, waiting for transfers between devices, body(): lax.all_to_all(inputs, 'fsdp', split_axis=1, concat_axis=0, tiled=True)  46.6 us
    all_gather x1, waiting for transfers between devices, body(): all_upstream = lax.all_gather(upstream, 'fsdp', axis=0, tiled=True)  41.1 us
    dot_general x16, matrix products, add_group(): lax.dot_general(pair[0], pair[1], (((0,), (0,)), ((), ())), preferred_ele...  27.5 us
    all_to_all x1, starting transfers between devices, body(): lax.all_to_all(inputs, 'fsdp', split_axis=1, concat_axis=0, tiled=True)  11.8 us
    broadcast_in_dim x1, other arithmetic, body(): return (momentum_next.astype(jnp.bfloat16), stepped[None])  5.25 us
  transfers between devices with their start and end apart: 3, of which 3 were waited for; matrix products, arithmetic and copies ran while one was open for 16% of the time, Pallas kernels for 0%

commit v1 on v0

--- a/solution.py
+++ b/solution.py
@@ -21,7 +21,7 @@
     dequant = (code_vals.astype(jnp.float32) * scales.astype(jnp.float32)).reshape(
         row_count, col_count
     )
-    outer_grad = lax.psum(dequant, "replica") / replicas
+    outer_grad = jnp.sum(lax.all_gather(dequant, "replica"), axis=0) / replicas
     momentum_next = momentum_decay * momentum + outer_grad
     renewed = base - outer_rate * (outer_grad + momentum_decay * momentum_next)
     tok_rows = tokens.shape[1]

time: 256 us -> 497 us (1.94)
  waiting for transfers between devices: 182 us -> 408 us
  other arithmetic: 12.4 us -> 27.9 us
    all_gather x0 -> x1, waiting for transfers between devices: none -> 325 us  [body(): outer_grad = jnp.sum(lax.all_gather(dequant, 'replica'), axis=0) / replicas]
    psum x1 -> x0, waiting for transfers between devices: 93.7 us -> none  [body(): outer_grad = lax.psum(dequant, 'replica') / replicas]
    reduce_sum x0 -> x1, other arithmetic: none -> 13.4 us  [body(): outer_grad = jnp.sum(lax.all_gather(dequant, 'replica'), axis=0) / replicas]
  transfers between devices with their start and end apart: 3 -> 3, of which waited for: 3 -> 3; matrix products, arithmetic and copies ran while one was open for 16% -> 9% of each run, Pallas kernels for 0% -> 0%
where the time goes in v1:
time: 497 us; the launch traced here: 495 us
  waiting for transfers between devices  408 us (82%)
  other arithmetic  27.9 us (6%)
  matrix products  27.5 us (6%)
  between operations  14.2 us (3%)
  starting transfers between devices  11.6 us (2%)
  local copies, waits for them, and re-layouts  5.9 us (1%)
    all_gather x1, waiting for transfers between devices, body(): outer_grad = jnp.sum(lax.all_gather(dequant, 'replica'), axis=0) / replicas  325 us
    all_to_all x1, waiting for transfers between devices, body(): lax.all_to_all(inputs, 'fsdp', split_axis=1, concat_axis=0, tiled=True)  44.4 us
    all_gather x1, waiting for transfers between devices, body(): all_upstream = lax.all_gather(upstream, 'fsdp', axis=0, tiled=True)  37.3 us
    dot_general x16, matrix products, add_group(): lax.dot_general(pair[0], pair[1], (((0,), (0,)), ((), ())), preferred_ele...  27.5 us
    reduce_sum x1, other arithmetic, body(): outer_grad = jnp.sum(lax.all_gather(dequant, 'replica'), axis=0) / replicas  13.4 us
    all_to_all x1, starting transfers between devices, body(): lax.all_to_all(inputs, 'fsdp', split_axis=1, concat_axis=0, tiled=True)  11.6 us
  transfers between devices with their start and end apart: 3, of which 3 were waited for; matrix products, arithmetic and copies ran while one was open for 9% of the time, Pallas kernels for 0%

profile of v1, /device:TPU:8, one launch (start us, length us, event | category | flops | bytes accessed | tf_op | source)
XLA Modules:
  0.0 495.2 jit_solution(13002094018844573031)
XLA Ops:
  7.9 2.2 abs_bitcast_fusion
  10.1 1.8 copy.21
  11.9 2.4 reduce_max.9
  15.2 2.2 bitcast_multiply_fusion
  17.4 3.2 copy.18
  20.9 2.3 broadcast_select_fusion
  23.2 11.6 %all-to-all-start = ((bf16[128,16,512]{0,2,1:T(8,128)(2,1)}), bf16[128,16,512]{0,2,1:T(8,128)(2,1)}, u32[]{:S(2)}, u32[]{:S(2)}) async-start(bf16[128,16,512]{0,2,1:T(8,128)(2,1)} %broadcast_select_fusion), calls=%async_computation | async-start | bytes 4194304 | tf_op jit(solution)/shard_map/all_to_all | solution.py:39
  34.8 44.4 %all-to-all-done = bf16[128,16,512]{0,2,1:T(8,128)(2,1)} async-done(((bf16[128,16,512]{0,2,1:T(8,128)(2,1)}), bf16[128,16,512]{0,2,1:T(8,128)(2,1)}, u32[]{:S(2)}, u32[]{:S(2)}) %all-to-all-start) | async-done | bytes 2097184 | tf_op jit(solution)/shard_map/all_to_all | solution.py:39
  79.2 37.3 %all-gather.7.cloned.1.call-done = bf16[1,2048,1024]{2,1,0:T(8,128)(2,1)} async-done(((bf16[1,128,1024]{2,1,0:T(8,128)(2,1)}), bf16[1,2048,1024]{2,1,0:T(8,128)(2,1)}) %all-gather.7.cloned.1.call-update) | async-done | bytes 4194320 | tf_op jit(solution)/shard_map/all_gather | solution.py:40
  116.4 27.9 %while.11 = (s32[]{:T(128)}, f32[512,1024]{1,0:T(8,128)S(1)}, bf16[16,128,512]{1,2,0:T(8,128)(2,1)}, bf16[16,128,1024]{2,1,0:T(8,128)(2,1)}, s32[]{:T(128)}, /*index=5*/s32[]{:T(128)}) while((s32[]{:T(128)}, f32[512,1024]{1,0:T(8,128)S(1)}, bf16[16,128,512]{1,2,0:T(8,128)(2,1)}, bf16[16,128,1024]{2,1,0:T(8,128)(2,1)}, s32[]{:T(128)}, ...), condition=%wide.region_4.5_spmd.clone, body=%wide.region_3.4_spmd.clone.sunk | while | flops 136314880 | bytes 4588623 | solution.py:51
  119.9 1.7 select_add_fusion.2
  121.7 1.7 select_add_fusion.2
  123.4 1.7 select_add_fusion.2
  125.1 1.8 select_add_fusion.2
  126.9 1.8 select_add_fusion.2
  128.7 1.7 select_add_fusion.2
  132.2 1.7 select_add_fusion.2
  133.9 1.7 select_add_fusion.2
  137.4 1.7 select_add_fusion.2
  139.1 1.7 select_add_fusion.2
  142.6 1.7 select_add_fusion.2
  144.4 325.3 %all-gather.5.cloned.1.call-done = f32[8192,1024]{1,0:T(8,128)} async-done(((f32[512,1024]{1,0:T(8,128)}), f32[8192,1024]{1,0:T(8,128)}) %all-gather.5.cloned.1.call-update) | async-done | bytes 33554448 | tf_op jit(solution)/shard_map/all_gather | solution.py:24
  469.7 13.4 %reduce_sum.9 = f32[512,1024]{1,0:T(8,128)} reduce(f32[16,512,1024]{2,1,0:T(8,128)} %bitcast.32, f32[]{:T(128)} %constant.52.clone.1), dimensions={0}, to_apply=%region_1.0 | reduce | flops 7864320 | bytes 35651588 | tf_op jit(solution)/shard_map/reduce_sum | solution.py:24
  483.1 5.3 %fusion.7 = (bf16[1,512,1024]{2,1,0:T(8,128)(2,1)}, bf16[512,1024]{1,0:T(8,128)(2,1)}) fusion(f32[512,1024]{1,0:T(8,128)S(1)} %get-tuple-element.24, f32[512,1024]{1,0:T(8,128)} %param.9, f32[512,1024]{1,0:T(8,128)} %param.11, f32[512,1024]{1,0:T(8,128)} %reduce_sum.9), kind=kLoop, calls=%fused_computation.16 | loop fusion | flops 5767168 | bytes 10485760 | tf_op jit(solution)/shard_map/broadcast_in_dim | solution.py:56
  (27 shorter events, 10.5 us)
Async XLA Ops:
  7.2 109.3 %all-gather.7.cloned.1.call-start = ((), (), s32[]{:S(2)}) async-start(), calls=%async_computation.2 | async-start | bytes 4456448 | tf_op jit(solution)/shard_map/all_gather | solution.py:40
  7.9 461.8 %all-gather.5.cloned.1.call-start = ((), (), s32[]{:S(2)}) async-start(), calls=%async_computation.1 | async-start | bytes 35651584 | tf_op jit(solution)/shard_map/all_gather | solution.py:24
  11.9 3.2 copy-start
  11.9 3.2 copy-start.1
  17.4 3.3 copy-start.2
  17.4 3.3 copy-start.3
  23.2 56.0 %all-to-all-start = ((bf16[128,16,512]{0,2,1:T(8,128)(2,1)}), bf16[128,16,512]{0,2,1:T(8,128)(2,1)}, u32[]{:S(2)}, u32[]{:S(2)}) async-start(bf16[128,16,512]{0,2,1:T(8,128)(2,1)} %broadcast_select_fusion), calls=%async_computation | async-start | bytes 4194304 | tf_op jit(solution)/shard_map/all_to_all | solution.py:39
Sparse Core Ops, SparseCore 0:
  10.7 105.7 all-gather.6
  118.2 351.3 all-gather.4

commit v2 on v0

--- a/solution.py
+++ b/solution.py
@@ -37,7 +37,9 @@
     inputs = jnp.where(masked[:, None], mask_embed[None, :], tokens[0])
     upstream = cotangent[0]
     own_columns = lax.all_to_all(inputs, "fsdp", split_axis=1, concat_axis=0, tiled=True)
-    all_upstream = lax.all_gather(upstream, "fsdp", axis=0, tiled=True)
+    all_upstream = jnp.concatenate(
+        lax.all_to_all(jnp.stack([upstream] * lax.axis_size("fsdp")), "fsdp", 0, 0), axis=0
+    )
     groups = lax.axis_size("fsdp")
     group_in = own_columns.reshape(groups, tok_rows, row_count)
     group_up = all_upstream.reshape(groups, tok_rows, col_count)

time: 256 us -> 311 us (1.21)
  blocking collectives: 0 us -> 51.2 us
  starting transfers between devices: 11.9 us -> 18.5 us
  waiting for transfers between devices: 182 us -> 178 us
    all_to_all x0 -> x1, blocking collectives: none -> 51.2 us  [body(): lax.all_to_all(inputs, 'fsdp', split_axis=1, concat_axis=0, tiled=True)]
    all_gather x1 -> x0, waiting for transfers between devices: 41.1 us -> none  [body(): all_upstream = lax.all_gather(upstream, 'fsdp', axis=0, tiled=True)]
    psum x1, waiting for transfers between devices: 93.7 us -> 123 us  [body(): outer_grad = lax.psum(dequant, 'replica') / replicas]
    all_to_all x1, waiting for transfers between devices: 46.6 us -> 55.4 us  [body(): lax.all_to_all(jnp.stack([upstream] * lax.axis_size('fsdp')), 'fsdp', 0, 0)]
    all_to_all x1, starting transfers between devices: 11.8 us -> 18.4 us  [body(): lax.all_to_all(jnp.stack([upstream] * lax.axis_size('fsdp')), 'fsdp', 0, 0)]
  transfers between devices with their start and end apart: 3 -> 2, of which waited for: 3 -> 2; matrix products, arithmetic and copies ran while one was open for 16% -> 11% of each run, Pallas kernels for 0% -> 0%
where the time goes in v2:
time: 311 us; the launch traced here: 310 us
  waiting for transfers between devices  178 us (57%)
  blocking collectives  51.2 us (16%)
  matrix products  27.5 us (9%)
  starting transfers between devices  18.5 us (6%)
  between operations  14.2 us (5%)
  other arithmetic  11.7 us (4%)
  local copies, waits for them, and re-layouts  8.38 us (3%)
    psum x1, waiting for transfers between devices, body(): outer_grad = lax.psum(dequant, 'replica') / replicas  123 us
    all_to_all x1, waiting for transfers between devices, body(): lax.all_to_all(jnp.stack([upstream] * lax.axis_size('fsdp')), 'fsdp', 0, 0)  55.4 us
    all_to_all x1, blocking collectives, body(): lax.all_to_all(inputs, 'fsdp', split_axis=1, concat_axis=0, tiled=True)  51.2 us
    dot_general x16, matrix products, add_group(): lax.dot_general(pair[0], pair[1], (((0,), (0,)), ((), ())), preferred_ele...  27.5 us
    all_to_all x1, starting transfers between devices, body(): lax.all_to_all(jnp.stack([upstream] * lax.axis_size('fsdp')), 'fsdp', 0, 0)  18.4 us
  transfers between devices with their start and end apart: 2, of which 2 were waited for; matrix products, arithmetic and copies ran while one was open for 11% of the time, Pallas kernels for 0%

profile of v2, /device:TPU:8, one launch (start us, length us, event | category | flops | bytes accessed | tf_op | source)
XLA Modules:
  0.0 310.0 jit_solution(14918062218840260866)
XLA Ops:
  7.2 3.2 %copy.18 = bf16[1,128,8192]{1,2,0:T(8,128)(2,1)S(1)} copy(bf16[1,128,8192]{2,1,0:T(8,128)(2,1)} %param.12) | data formatting | bytes 4194304 | tf_op args[3]
  12.2 51.2 %all_to_all.18 = bf16[128,16,512]{0,2,1:T(8,128)(2,1)} all-to-all(bf16[128,16,512]{0,2,1:T(8,128)(2,1)S(1)} %broadcast_select_fusion), channel_id=1, replica_groups=mesh['replica'=16,'fsdp'=16] {'fsdp'}, dimensions={1} | all-to-all | bytes 4194304 | tf_op jit(solution)/shard_map/all_to_all | solution.py:39
  63.4 2.5 stack.3
  65.9 18.4 %all-to-all-start.1 = ((bf16[16,128,1024]{2,1,0:T(8,128)(2,1)}), bf16[16,128,1024]{2,1,0:T(8,128)(2,1)}, u32[]{:S(2)}, u32[]{:S(2)}) async-start(bf16[16,128,1024]{2,1,0:T(8,128)(2,1)} %stack.3), calls=%async_computation.1 | async-start | bytes 8388608 | tf_op jit(solution)/shard_map/all_to_all | solution.py:41
  84.8 1.8 copy.21
  86.5 2.2 reduce_max.9
  89.6 2.2 bitcast_multiply_fusion
  91.8 55.4 %all-to-all-done.1 = bf16[16,128,1024]{2,1,0:T(8,128)(2,1)} async-done(((bf16[16,128,1024]{2,1,0:T(8,128)(2,1)}), bf16[16,128,1024]{2,1,0:T(8,128)(2,1)}, u32[]{:S(2)}, u32[]{:S(2)}) %all-to-all-start.1) | async-done | bytes 4194336 | tf_op jit(solution)/shard_map/all_to_all | solution.py:41
  147.3 27.8 %while.11 = (s32[]{:T(128)}, f32[512,1024]{1,0:T(8,128)S(1)}, bf16[16,128,512]{1,2,0:T(8,128)(2,1)}, bf16[16,128,1024]{2,1,0:T(8,128)(2,1)}, s32[]{:T(128)}, /*index=5*/s32[]{:T(128)}) while((s32[]{:T(128)}, f32[512,1024]{1,0:T(8,128)S(1)}, bf16[16,128,512]{1,2,0:T(8,128)(2,1)}, bf16[16,128,1024]{2,1,0:T(8,128)(2,1)}, s32[]{:T(128)}, ...), condition=%wide.region_4.5_spmd.clone, body=%wide.region_3.4_spmd.clone.sunk | while | flops 136314880 | bytes 4588623 | solution.py:53
  149.0 1.7 select_add_fusion.2
  150.7 1.7 select_add_fusion.2
  152.5 1.7 select_add_fusion.2
  154.2 1.7 select_add_fusion.2
  156.0 1.7 select_add_fusion.2
  157.7 1.7 select_add_fusion.2
  159.5 1.7 select_add_fusion.2
  161.2 1.7 select_add_fusion.2
  162.9 1.7 select_add_fusion.2
  166.4 1.7 select_add_fusion.2
  168.2 1.7 select_add_fusion.2
  171.6 1.7 select_add_fusion.2
  173.4 1.7 select_add_fusion.2
  175.1 122.8 %all-reduce.2.cloned.1.call-done = f32[512,1024]{1,0:T(8,128)} async-done(((f32[512,1024]{1,0:T(8,128)}), f32[512,1024]{1,0:T(8,128)}) %all-reduce.2.cloned.1.call-update) | async-done | bytes 2097168 | tf_op jit(solution)/shard_map/psum | solution.py:24
  297.9 5.3 %fusion.7 = (bf16[1,512,1024]{2,1,0:T(8,128)(2,1)}, bf16[512,1024]{1,0:T(8,128)(2,1)}) fusion(f32[512,1024]{1,0:T(8,128)S(1)} %get-tuple-element.24, f32[512,1024]{1,0:T(8,128)} %param.9, f32[512,1024]{1,0:T(8,128)} %param.11, f32[512,1024]{1,0:T(8,128)} %all-reduce.2.cloned.1.call-done), kind=kLoop, calls=%fused_computation.16 | loop fusion | flops 5767168 | bytes 10485760 | tf_op jit(solution)/shard_map/broadcast_in_dim | solution.py:58
  (27 shorter events, 8.2 us)
Async XLA Ops:
  7.2 3.3 %copy-start.3 = (bf16[8192]{0:T(1024)(128)(2,1)S(1)}, bf16[8192]{0:T(1024)(128)(2,1)}, u32[]{:S(2)}) copy-start(bf16[8192]{0:T(1024)(128)(2,1)} %param.13) | copy-start | bytes 49156
  7.2 3.3 %copy-start.4 = (s32[1,1,768]{2,1,0:T(1,128)S(1)}, s32[1,1,768]{2,1,0:T(1,128)}, u32[]{:S(2)}) copy-start(s32[1,1,768]{2,1,0:T(1,128)} %param.14) | copy-start | bytes 9220
  12.2 51.2 %copy-start.2 = (bf16[1,128,1024]{2,1,0:T(8,128)(2,1)S(1)}, bf16[1,128,1024]{2,1,0:T(8,128)(2,1)}, u32[]{:S(2)}) copy-start(bf16[1,128,1024]{2,1,0:T(8,128)(2,1)} %param.15) | copy-start | bytes 786436
  65.9 18.5 %copy-start = (f32[512,1024]{1,0:T(8,128)S(1)}, f32[512,1024]{1,0:T(8,128)}, u32[]{:S(2)}) copy-start(f32[512,1024]{1,0:T(8,128)} %param.9) | copy-start | bytes 6291460
  65.9 18.5 %copy-start.1 = (bf16[1,512,1024]{2,1,0:T(8,128)(2,1)S(1)}, bf16[1,512,1024]{2,1,0:T(8,128)(2,1)}, u32[]{:S(2)}) copy-start(bf16[1,512,1024]{2,1,0:T(8,128)(2,1)} %param.10) | copy-start | bytes 3145732
  65.9 81.3 %all-to-all-start.1 = ((bf16[16,128,1024]{2,1,0:T(8,128)(2,1)}), bf16[16,128,1024]{2,1,0:T(8,128)(2,1)}, u32[]{:S(2)}, u32[]{:S(2)}) async-start(bf16[16,128,1024]{2,1,0:T(8,128)(2,1)} %stack.3), calls=%async_computation.1 | async-start | bytes 8388608 | tf_op jit(solution)/shard_map/all_to_all | solution.py:41
  84.4 213.6 %all-reduce.2.cloned.1.call-start = ((), (), s32[]{:S(2)}) async-start(), calls=%async_computation.2 | async-start | bytes 4194304 | tf_op jit(solution)/shard_map/psum | solution.py:24
Sparse Core Ops, SparseCore 0:
  91.9 205.9 all-reduce.1
